TPU v7x, 128 devices: a whole 4x4x4 slice. The times are simulated.
128 devices in a mesh: req: 8 (over y, core), tok: 16 (over x, z).
Axes of the slice: x: 4, y: 4, z: 4, core: 2. Of those that a mesh axis runs over, the one named last changes fastest.
Arguments:
- layer_input: bfloat16 [16384, 2048], P(('req', 'tok')), may hold values from -12 to 12
- q_in: bfloat16 [16384, 2048], P(('req', 'tok')), may hold values from -10 to 10
- k_in: bfloat16 [16384, 2048], P(('req', 'tok')), may hold values from -10 to 10
- v_in: bfloat16 [16384, 2048], P(('req', 'tok')), may hold values from -6 to 6
- segment_ids: int32 [8, 2048], P('req'), may hold values from 0 to 3, never falling along the last dimension, each value on 1 to 1024 neighbouring positions
- lambda_parts: float32 [4, 128], replicated, may hold values from -0.8 to 0.8
- out_weight: bfloat16 [2048, 2048], replicated, may hold values from -0.125 to 0.125
- ffn_gain: float32 [2048], replicated, may hold values from 0.1 to 1.9
- gate_weight: bfloat16 [2048, 5632], P(None, 'req'), may hold values from -0.125 to 0.125
- up_weight: bfloat16 [2048, 5632], P(None, 'req'), may hold values from -0.125 to 0.125
- down_weight: bfloat16 [5632, 2048], P('req'), may hold values from -0.078125 to 0.078125
- next_gain: float32 [2048], replicated, may hold values from 0.1 to 1.9
- qkv_weight: bfloat16 [2048, 6144], P(None, 'req'), may hold values from -0.125 to 0.125
- page_owner: int32 [8, 256], P('req'), may hold values from 0 to 15, as said below
- page_slot: int32 [8, 256], P('req'), may hold values from 0 to 15, as said below
Outputs:
- layer_output: bfloat16 [16384, 2048], P(('req', 'tok'))
- q_next: bfloat16 [16384, 2048], P(('req', 'tok'))
- page_cache: bfloat16 [2048, 8, 4096], P(('req', 'tok'))
Inputs may be any that keep to these rules, and one draw needn't show every extreme that they name: `segment_ids`: segment numbers never fall along a group; each of the 4 prompts of a group has 1 to 1024 tokens, one exactly 1024. `page_owner`: the 16 pages of each device name every device of its request group as owner exactly once. `page_slot`: within a request group every pair of owner and slot is named by exactly one page.
All inputs are finite; a program needn't handle non-finite values.
Results may differ from a plain program's by a relative error of at most 0.017.
Values may be sent and summed in bfloat16 or wider, within the bound.
A program may use at most 192 MiB of HBM per device.

v0:
```python
import math
import jax
import jax.numpy as jnp
from jax import lax
from jax.sharding import PartitionSpec as P

HEADS = 8
PAGE = 8
NEG_FILL = -1e30
LAMBDA_INIT = 0.2
EPSILON = 1e-05


def rms_rows(values):
    return values * lax.rsqrt(jnp.mean(values * values, axis=-1, keepdims=True) + EPSILON)


def lambda_value(lambda_parts):
    first_term = jnp.exp(jnp.sum(lambda_parts[0] * lambda_parts[1]))
    second_term = jnp.exp(jnp.sum(lambda_parts[2] * lambda_parts[3]))
    return first_term - second_term + LAMBDA_INIT


def body(
    layer_input,
    q_in,
    k_in,
    v_in,
    segment_ids,
    lambda_parts,
    out_weight,
    ffn_gain,
    gate_weight,
    up_weight,
    down_weight,
    next_gain,
    qkv_weight,
    page_owner,
    page_slot,
):
    row_count = q_in.shape[0]
    feat_width = q_in.shape[1]
    head_dim = feat_width // (2 * HEADS)
    peer_count = lax.axis_size("tok")
    tok_place = lax.axis_index("tok")
    seg_row = segment_ids[0]
    first_row = tok_place * row_count
    query_places = first_row + jnp.arange(row_count)
    query_segs = lax.dynamic_slice_in_dim(seg_row, first_row, row_count)
    lambda_mix = lambda_value(lambda_parts)
    score_scale = 1.0 / math.sqrt(head_dim)
    query_split = q_in.reshape(row_count, HEADS, 2, head_dim)
    run_max = jnp.full((HEADS, 2, row_count), NEG_FILL, jnp.float32)
    key_rows = lax.all_gather(k_in, "tok", axis=0, tiled=True)
    value_rows = lax.all_gather(v_in, "tok", axis=0, tiled=True)
    piece_len = key_rows.shape[0]
    key_split = key_rows.reshape(piece_len, HEADS, 2, head_dim)
    value_split = value_rows.reshape(piece_len, HEADS, 2 * head_dim)
    key_places = jnp.arange(piece_len)
    visible = (seg_row[None, :] == query_segs[:, None]) & (
        key_places[None, :] <= query_places[:, None]
    )
    scores = (
        jnp.einsum("qhmd,khmd->hmqk", query_split, key_split, preferred_element_type=jnp.float32)
        * score_scale
    )
    scores = jnp.where(visible, scores, NEG_FILL)
    new_max = jnp.maximum(run_max, jnp.max(scores, axis=-1))
    weights = jnp.where(visible, jnp.exp(scores - new_max[..., None]), 0.0)
    totals = jnp.sum(weights, axis=-1)
    weighted = jnp.einsum(
        "hmqk,khe->hmqe",
        weights.astype(jnp.bfloat16),
        value_split,
        preferred_element_type=jnp.float32,
    )
    run_max, totals, weighted = (new_max, totals, weighted)
    map_outputs = weighted / totals[..., None]
    difference = map_outputs[:, 0] - lambda_mix * map_outputs[:, 1]
    head_outputs = rms_rows(difference) * (1.0 - LAMBDA_INIT)
    attention = (
        jnp.transpose(head_outputs, (1, 0, 2)).reshape(row_count, feat_width).astype(jnp.bfloat16)
    )
    residual_mid = (
        layer_input.astype(jnp.float32)
        + jnp.dot(attention, out_weight, preferred_element_type=jnp.float32)
    ).astype(jnp.bfloat16)
    gathered = lax.all_gather(residual_mid, "req", axis=0, tiled=True)
    normed = (rms_rows(gathered.astype(jnp.float32)) * ffn_gain).astype(jnp.bfloat16)
    gate_proj = jnp.dot(normed, gate_weight, preferred_element_type=jnp.float32)
    up_proj = jnp.dot(normed, up_weight, preferred_element_type=jnp.float32)
    hidden = (jax.nn.silu(gate_proj) * up_proj).astype(jnp.bfloat16)
    ffn_own = lax.psum_scatter(
        jnp.dot(hidden, down_weight, preferred_element_type=jnp.float32).astype(jnp.bfloat16),
        "req",
        scatter_dimension=0,
        tiled=True,
    ).astype(jnp.float32)
    layer_output = (residual_mid.astype(jnp.float32) + ffn_own).astype(jnp.bfloat16)
    next_normed = (rms_rows(layer_output.astype(jnp.float32)) * next_gain).astype(jnp.bfloat16)
    projected_cols = jnp.dot(
        lax.all_gather(next_normed, "req", axis=0, tiled=True),
        qkv_weight,
        preferred_element_type=jnp.float32,
    ).astype(jnp.bfloat16)
    projected = lax.all_to_all(projected_cols, "req", split_axis=0, concat_axis=1, tiled=True)
    q_next = projected[:, :feat_width]
    pages_dev = row_count // PAGE
    per_owner = pages_dev // peer_count
    key_values = projected[:, feat_width:].reshape(pages_dev, PAGE, 2 * feat_width)
    owner_all = page_owner[0].reshape(peer_count, pages_dev)
    slot_all = page_slot[0].reshape(peer_count, pages_dev)
    page_numbers = jnp.arange(pages_dev, dtype=jnp.int32)
    my_owners = lax.dynamic_index_in_dim(owner_all, tok_place, 0, keepdims=False)
    send_order = jnp.argsort(my_owners * pages_dev + page_numbers)
    outgoing = key_values[send_order].reshape(peer_count, per_owner, PAGE, 2 * feat_width)
    incoming = lax.all_to_all(outgoing, "tok", split_axis=0, concat_axis=0, tiled=True)
    rank_keys = jnp.where(
        owner_all == tok_place, page_numbers[None, :], pages_dev + page_numbers[None, :]
    )
    chosen_pages = jnp.argsort(rank_keys, axis=1)[:, :per_owner]
    slot_list = jnp.take_along_axis(slot_all, chosen_pages, axis=1).reshape(pages_dev)
    page_cache = (
        jnp.zeros((pages_dev, PAGE, 2 * feat_width), jnp.bfloat16)
        .at[slot_list]
        .set(incoming.reshape(pages_dev, PAGE, 2 * feat_width))
    )
    return (layer_output, q_next, page_cache)


def solution(mesh):
    in_specs = (
        P(("req", "tok"), None),
        P(("req", "tok"), None),
        P(("req", "tok"), None),
        P(("req", "tok"), None),
        P("req", None),
        P(),
        P(),
        P(),
        P(None, "req"),
        P(None, "req"),
        P("req", None),
        P(),
        P(None, "req"),
        P("req", None),
        P("req", None),
    )
    out_specs = (P(("req", "tok"), None), P(("req", "tok"), None), P(("req", "tok"), None, None))
    return jax.shard_map(body, mesh=mesh, in_specs=in_specs, out_specs=out_specs, check_vma=False)
```

profile of v0, /device:TPU:0, one launch (start us, length us, event | category | flops | bytes accessed | tf_op | source)
XLA Modules:
  0.0 395.1 jit_solution(589856986905657744)
XLA Ops:
  7.2 2.2 copy.35
  9.5 2.0 copy.38
  11.6 2.2 reshape.96
  16.2 75.5 %all-gather.5.cloned.1.call-done = bf16[2048,2048]{0,1:T(8,128)(2,1)} async-done(((bf16[128,2048]{0,1:T(8,128)(2,1)}), bf16[2048,2048]{0,1:T(8,128)(2,1)}) %all-gather.5.cloned.1.call-update) | async-done | bytes 8388624 | tf_op jit(solution)/shard_map/all_gather | solution.py:54
  91.7 6.6 %fusion = (f32[8,2,128]{2,1,0:T(2,128)S(1)}, f32[8,2,128,2048]{3,2,1,0:T(8,128)S(1)}) fusion(pred[128,2048]{1,0:T(8,128)(4,1)S(1)} %fusion.24, bf16[2048,8,2,128]{0,3,2,1:T(8,128)(2,1)} %bitcast.49, bf16[128,8,2,128]{3,2,1,0:T(2,128)(2,1)} %reshape.96), kind=kOutput, calls=%fused_computation.5 | convolution fusion | flops 1086322688 | bytes 25960448 | tf_op jit(solution)/shard_map/qhmd,khmd->hmqk/dot_general | solution.py:64
  98.4 5.9 %copy-done.1 = f32[8,2,128,2048]{3,2,1,0:T(8,128)} copy-done((f32[8,2,128,2048]{3,2,1,0:T(8,128)}, f32[8,2,128,2048]{3,2,1,0:T(8,128)S(1)}, u32[]{:S(2)}) %copy-start.1) | copy-done | bytes 16777240
  104.3 5.0 %fusion.1 = f32[8,2,128]{2,1,0:T(2,128)S(1)} fusion(f32[8,2,128,2048]{3,2,1,0:T(8,128)S(1)} %get-tuple-element.12, f32[8,2,128]{2,1,0:T(2,128)S(1)} %broadcast_maximum_fusion, pred[128,2048]{1,0:T(8,128)(4,1)S(1)} %fusion.24), kind=kLoop, calls=%fused_computation.6 | loop fusion | flops 20969472 | bytes 17055744 | tf_op jit(solution)/shard_map/reduce_sum | solution.py:70
  109.3 63.0 %all-gather.7.cloned.1.call-done = bf16[2048,2048]{0,1:T(8,128)(2,1)} async-done(((bf16[128,2048]{0,1:T(8,128)(2,1)}), bf16[2048,2048]{0,1:T(8,128)(2,1)}) %all-gather.7.cloned.1.call-update) | async-done | bytes 8388624 | tf_op jit(solution)/shard_map/all_gather | solution.py:55
  172.3 12.6 %broadcast_divide_fusion = f32[8,2,128,256]{3,2,1,0:T(8,128)S(1)} fusion(f32[8,2,128]{2,1,0:T(2,128)S(1)} %fusion.1, bf16[2048,8,256,1]{0,2,3,1:T(8,128)(2,1)} %bitcast.56, f32[8,2,128,2048]{3,2,1,0:T(8,128)} %copy-done.1, f32[8,2,128]{2,1,0:T(2,128)S(1)} %broadcast_maximum_fusion, pred[128,2048]{1,0:T(8,128)(4,1)S(1)} %fusion.24), kind=kOutput, calls=%fused_computation.37 | convolution fusion | flops 2168979456 | bytes 27541504 | tf_op jit(solution)/shard_map/hmqk,khe->hmqe/dot_general | solution.py:71
  185.1 1.1 fusion.25
  186.2 2.0 copy.40
  188.3 5.7 %fusion.13 = bf16[128,2048]{1,0:T(8,128)(2,1)} fusion(bf16[128,2048]{0,1:T(8,128)(2,1)} %bitcast.53, bf16[2048,2048]{1,0:T(8,128)(2,1)} %param.21, bf16[128,2048]{1,0:T(8,128)(2,1)} %param.15), kind=kOutput, calls=%fused_computation.22 | convolution fusion | flops 1074528256 | bytes 9961472 | tf_op jit(solution)/shard_map/dot_general | solution.py:86
  194.2 31.3 %all-gather.9.cloned.1.call-done = bf16[1024,2048]{1,0:T(8,128)(2,1)} async-done(((bf16[128,2048]{1,0:T(8,128)(2,1)}), bf16[1024,2048]{1,0:T(8,128)(2,1)}) %all-gather.9.cloned.1.call-update) | async-done | bytes 4194320 | tf_op jit(solution)/shard_map/all_gather | solution.py:88
  225.5 3.2 fusion.3
  228.9 6.7 %fusion.15 = f32[1024,704]{0,1:T(8,128)} fusion(bf16[2048,704]{0,1:T(8,128)(2,1)} %param.23, bf16[1024,2048]{1,0:T(8,128)(2,1)S(1)} %copy-done.3, f32[2048]{0:T(1024)S(1)} %copy-done.10, f32[1024]{0:T(1024)S(1)} %add_rsqrt_fusion), kind=kOutput, calls=%fused_computation.26 | convolution fusion | flops 2961178624 | bytes 9973760 | tf_op jit(solution)/shard_map/dot_general | solution.py:90
  235.7 12.4 %convolution_convert_fusion = bf16[1024,2048]{1,0:T(8,128)(2,1)} fusion(bf16[704,2048]{1,0:T(8,128)(2,1)} %param.25, f32[1024,704]{0,1:T(8,128)} %fusion.15, bf16[2048,704]{0,1:T(8,128)(2,1)} %param.24, bf16[1024,2048]{1,0:T(8,128)(2,1)} %all-gather.9.cloned.1.call-done, f32[2048]{0:T(1024)S(1)} %copy-done.10, f32[1024]{0:T(1024)S(1)} %add_rsqrt_fusion), kind=kOutput, calls=%fused_computation.19 | convolution fusion | flops 5920391168 | bytes 17051648 | tf_op jit(solution)/shard_map/dot_general | solution.py:94
  248.1 37.9 %reduce-scatter.2.cloned.1.call-done = bf16[128,2048]{1,0:T(8,128)(2,1)} async-done(((bf16[1024,2048]{1,0:T(8,128)(2,1)}), bf16[128,2048]{1,0:T(8,128)(2,1)}) %reduce-scatter.2.cloned.1.call-update) | async-done | bytes 524304 | tf_op jit(solution)/shard_map/reduce_scatter | solution.py:93
  286.0 1.5 fusion.19
  289.3 31.2 %all-gather.11.cloned.1.call-done = bf16[1024,2048]{1,0:T(8,128)(2,1)} async-done(((bf16[128,2048]{1,0:T(8,128)(2,1)}), bf16[1024,2048]{1,0:T(8,128)(2,1)}) %all-gather.11.cloned.1.call-update) | async-done | bytes 4194320 | tf_op jit(solution)/shard_map/all_gather | solution.py:102
  320.4 6.8 %convolution_convert_fusion.1 = bf16[1024,768]{1,0:T(8,128)(2,1)} fusion(bf16[1024,2048]{1,0:T(8,128)(2,1)} %all-gather.11.cloned.1.call-done, bf16[2048,768]{1,0:T(8,128)(2,1)S(1)} %copy-done), kind=kOutput, calls=%fused_computation.23 | convolution fusion | flops 3222011904 | bytes 8912896 | tf_op jit(solution)/shard_map/dot_general | solution.py:101
  327.2 4.3 %all-to-all-start = ((bf16[8,128,768]{2,1,0:T(8,128)(2,1)}), bf16[8,128,768]{2,1,0:T(8,128)(2,1)}, u32[]{:S(2)}, u32[]{:S(2)}) async-start(bf16[8,128,768]{2,1,0:T(8,128)(2,1)} %bitcast.54), calls=%async_computation.1 | async-start | bytes 3145728 | tf_op jit(solution)/shard_map/all_to_all | solution.py:106
  333.6 1.2 sort.35
  334.9 18.2 %all-to-all-done = bf16[8,128,768]{2,1,0:T(8,128)(2,1)} async-done(((bf16[8,128,768]{2,1,0:T(8,128)(2,1)}), bf16[8,128,768]{2,1,0:T(8,128)(2,1)}, u32[]{:S(2)}, u32[]{:S(2)}) %all-to-all-start) | async-done | bytes 1572896 | tf_op jit(solution)/shard_map/all_to_all | solution.py:106
  353.1 1.6 copy.47
  354.7 1.1 copy-done.2
  355.8 1.0 slice_bitcast_fusion
  356.9 2.8 gather_fusion
  359.7 7.0 %all-to-all-start.1 = ((bf16[16,1,8,4096]{3,2,1,0:T(8,128)(2,1)}), bf16[16,1,8,4096]{3,2,1,0:T(8,128)(2,1)}, u32[]{:S(2)}, u32[]{:S(2)}) async-start(bf16[16,1,8,4096]{3,2,1,0:T(8,128)(2,1)} %bitcast.52), calls=%async_computation.2 | async-start | bytes 2097152 | tf_op jit(solution)/shard_map/all_to_all | solution.py:117
  368.2 1.9 slice.42
  370.1 14.1 %all-to-all-done.1 = bf16[16,1,8,4096]{3,2,1,0:T(8,128)(2,1)} async-done(((bf16[16,1,8,4096]{3,2,1,0:T(8,128)(2,1)}), bf16[16,1,8,4096]{3,2,1,0:T(8,128)(2,1)}, u32[]{:S(2)}, u32[]{:S(2)}) %all-to-all-start.1) | async-done | bytes 1048608 | tf_op jit(solution)/shard_map/all_to_all | solution.py:117
  384.1 1.1 broadcast_in_dim.54
  385.2 3.4 scatter_fusion
  (60 shorter events, 7.4 us)
Async XLA Ops:
  7.2 313.3 %copy-start = (bf16[2048,768]{1,0:T(8,128)(2,1)S(1)}, bf16[2048,768]{1,0:T(8,128)(2,1)}, u32[]{:S(2)}) copy-start(bf16[2048,768]{1,0:T(8,128)(2,1)} %param.27) | copy-start | bytes 9437188
  7.2 6.7 %copy-start.7 = (f32[4,128]{1,0:T(4,128)S(1)}, f32[4,128]{1,0:T(4,128)}, u32[]{:S(2)}) copy-start(f32[4,128]{1,0:T(4,128)} %param.20) | copy-start | bytes 6148
  7.2 8.6 %copy-start.6 = (s32[1,2048]{1,0:T(1,128)S(1)}, s32[1,2048]{1,0:T(1,128)}, u32[]{:S(2)}) copy-start(s32[1,2048]{1,0:T(1,128)} %param.19) | copy-start | bytes 24580
  7.2 84.5 %all-gather.5.cloned.1.call-start = ((), (), s32[]{:S(2)}) async-start(), calls=%async_computation.3 | async-start | bytes 8912896 | tf_op jit(solution)/shard_map/all_gather | solution.py:54
  9.5 162.8 %all-gather.7.cloned.1.call-start = ((), (), s32[]{:S(2)}) async-start(), calls=%async_computation.4 | async-start | bytes 8912896 | tf_op jit(solution)/shard_map/all_gather | solution.py:55
  11.6 213.9 %all-gather.9.cloned.1.call-start = ((), (), s32[]{:S(2)}) async-start(), calls=%async_computation.5 | async-start | bytes 4718592 | tf_op jit(solution)/shard_map/all_gather | solution.py:88
  98.4 5.9 %copy-start.1 = (f32[8,2,128,2048]{3,2,1,0:T(8,128)}, f32[8,2,128,2048]{3,2,1,0:T(8,128)S(1)}, u32[]{:S(2)}) copy-start(f32[8,2,128,2048]{3,2,1,0:T(8,128)S(1)} %get-tuple-element.12) | copy-start | bytes 50331652
  193.9 34.8 %copy-start.10 = (f32[2048]{0:T(1024)S(1)}, f32[2048]{0:T(1024)}, u32[]{:S(2)}) copy-start(f32[2048]{0:T(1024)} %param.22) | copy-start | bytes 24580
  193.9 92.0 %reduce-scatter.2.cloned.1.call-start = ((), (), s32[]{:S(2)}) async-start(), calls=%async_computation.6 | async-start | bytes 4718592 | tf_op jit(solution)/shard_map/reduce_scatter | solution.py:93
  225.5 3.4 copy-start.3
  248.1 40.2 %copy-start.5 = (f32[2048]{0:T(1024)S(1)}, f32[2048]{0:T(1024)}, u32[]{:S(2)}) copy-start(f32[2048]{0:T(1024)} %param.26) | copy-start | bytes 24580
  248.1 72.4 %all-gather.11.cloned.1.call-start = ((), (), s32[]{:S(2)}) async-start(), calls=%async_computation.7 | async-start | bytes 4718592 | tf_op jit(solution)/shard_map/all_gather | solution.py:102
  287.5 0.8 copy-start.4
  289.3 42.8 %copy-start.8 = (s32[1,256]{1,0:T(1,128)S(1)}, s32[1,256]{1,0:T(1,128)}, u32[]{:S(2)}) copy-start(s32[1,256]{1,0:T(1,128)} %param.28) | copy-start | bytes 3076
  289.3 43.6 %copy-start.9 = (s32[1,256]{1,0:T(1,128)S(1)}, s32[1,256]{1,0:T(1,128)}, u32[]{:S(2)}) copy-start(s32[1,256]{1,0:T(1,128)} %param.29) | copy-start | bytes 3076
  327.2 25.9 %all-to-all-start = ((bf16[8,128,768]{2,1,0:T(8,128)(2,1)}), bf16[8,128,768]{2,1,0:T(8,128)(2,1)}, u32[]{:S(2)}, u32[]{:S(2)}) async-start(bf16[8,128,768]{2,1,0:T(8,128)(2,1)} %bitcast.54), calls=%async_computation.1 | async-start | bytes 3145728 | tf_op jit(solution)/shard_map/all_to_all | solution.py:106
  354.7 1.2 copy-start.2
  359.7 24.4 %all-to-all-start.1 = ((bf16[16,1,8,4096]{3,2,1,0:T(8,128)(2,1)}), bf16[16,1,8,4096]{3,2,1,0:T(8,128)(2,1)}, u32[]{:S(2)}, u32[]{:S(2)}) async-start(bf16[16,1,8,4096]{3,2,1,0:T(8,128)(2,1)} %bitcast.52), calls=%async_computation.2 | async-start | bytes 2097152 | tf_op jit(solution)/shard_map/all_to_all | solution.py:117
Sparse Core Ops, SparseCore 0:
  10.7 80.9 all-gather.4
  94.4 77.8 all-gather.6
  194.1 31.3 all-gather.8
  248.2 37.7 reduce-scatter.1
  289.4 31.0 all-gather.10
where the time goes:
time: 396 us; the launch traced here: 395 us
  waiting for transfers between devices  271 us (68%)
  matrix products  50.8 us (13%)
  local copies, waits for them, and re-layouts  29.8 us (8%)
  other arithmetic  16.5 us (4%)
  between operations  15.3 us (4%)
  starting transfers between devices  11.7 us (3%)
    all_gather x1, waiting for transfers between devices, body(): key_rows = lax.all_gather(k_in, 'tok', axis=0, tiled=True)  75.5 us
    all_gather x1, waiting for transfers between devices, body(): value_rows = lax.all_gather(v_in, 'tok', axis=0, tiled=True)  63 us
    reduce_scatter x1, waiting for transfers between devices, body(): lax.psum_scatter(jnp.dot(hidden, down_weight, preferred_element_type=jnp....  37.9 us
    all_gather x1, waiting for transfers between devices, body(): gathered = lax.all_gather(residual_mid, 'req', axis=0, tiled=True)  31.3 us
    all_gather x1, waiting for transfers between devices, body(): lax.all_gather(next_normed, 'req', axis=0, tiled=True)  31.2 us
    all_to_all x1, waiting for transfers between devices, body(): lax.all_to_all(projected_cols, 'req', split_axis=0, concat_axis=1, tiled=...  18.2 us
    all_to_all x1, waiting for transfers between devices, body(): lax.all_to_all(outgoing, 'tok', split_axis=0, concat_axis=0, tiled=True)  14.1 us
    unnamed x26, local copies, waits for them, and re-layouts  12.8 us
  transfers between devices with their start and end apart: 7, of which 7 were waited for; matrix products, arithmetic and copies ran while one was open for 6% of the time, Pallas kernels for 0%

commit v1 on v0

--- a/solution.py
+++ b/solution.py
@@ -103,7 +103,12 @@
         qkv_weight,
         preferred_element_type=jnp.float32,
     ).astype(jnp.bfloat16)
-    projected = lax.all_to_all(projected_cols, "req", split_axis=0, concat_axis=1, tiled=True)
+    projected = jnp.concatenate(
+        lax.all_to_all(
+            jnp.stack(jnp.split(projected_cols, lax.axis_size("req"), axis=0)), "req", 0, 0
+        ),
+        axis=1,
+    )
     q_next = projected[:, :feat_width]
     pages_dev = row_count // PAGE
     per_owner = pages_dev // peer_count

time: 396 us -> 404 us (1.020)
  local copies, waits for them, and re-layouts: 29.8 us -> 40.6 us
    unnamed x26 -> x32, local copies, waits for them, and re-layouts: 12.8 us -> 18.5 us
    slice x0 -> x2, local copies, waits for them, and re-layouts: none -> 4.52 us  [body(): projected[:, feat_width:].reshape(pages_dev, PAGE, 2 * feat_width)]
where the time goes in v1:
time: 404 us; the launch traced here: 403 us
  waiting for transfers between devices  269 us (67%)
  matrix products  49.6 us (12%)
  local copies, waits for them, and re-layouts  40.6 us (10%)
  other arithmetic  16.5 us (4%)
  between operations  15.3 us (4%)
  starting transfers between devices  11.7 us (3%)
    all_gather x1, waiting for transfers between devices, body(): key_rows = lax.all_gather(k_in, 'tok', axis=0, tiled=True)  75.5 us
    all_gather x1, waiting for transfers between devices, body(): value_rows = lax.all_gather(v_in, 'tok', axis=0, tiled=True)  63 us
    reduce_scatter x1, waiting for transfers between devices, body(): lax.psum_scatter(jnp.dot(hidden, down_weight, preferred_element_type=jnp....  37.9 us
    all_gather x1, waiting for transfers between devices, body(): gathered = lax.all_gather(residual_mid, 'req', axis=0, tiled=True)  31.3 us
    all_gather x1, waiting for transfers between devices, body(): lax.all_gather(next_normed, 'req', axis=0, tiled=True)  31.2 us
    unnamed x32, local copies, waits for them, and re-layouts  18.5 us
    all_to_all x1, waiting for transfers between devices, body(): lax.all_to_all(jnp.stack(jnp.split(projected_cols, lax.axis_size('req'),...  18.2 us
    dot_general x1, matrix products, body(): jnp.einsum('hmqk,khe->hmqe', weights.astype(jnp.bfloat16), value_split, p...  12.6 us
  transfers between devices with their start and end apart: 7, of which 7 were waited for; matrix products, arithmetic and copies ran while one was open for 6% of the time, Pallas kernels for 0%

profile of v1, /device:TPU:0, one launch (start us, length us, event | category | flops | bytes accessed | tf_op | source)
XLA Modules:
  0.0 402.8 jit_solution(12794447956444543740)
XLA Ops:
  7.2 2.2 copy.37
  9.5 2.0 copy.40
  11.6 2.2 reshape.99
  16.2 75.5 %all-gather.5.cloned.1.call-done = bf16[2048,2048]{0,1:T(8,128)(2,1)} async-done(((bf16[128,2048]{0,1:T(8,128)(2,1)}), bf16[2048,2048]{0,1:T(8,128)(2,1)}) %all-gather.5.cloned.1.call-update) | async-done | bytes 8388624 | tf_op jit(solution)/shard_map/all_gather | solution.py:54
  91.7 6.6 %fusion = (f32[8,2,128]{2,1,0:T(2,128)S(1)}, f32[8,2,128,2048]{3,2,1,0:T(8,128)S(1)}) fusion(pred[128,2048]{1,0:T(8,128)(4,1)S(1)} %fusion.24, bf16[2048,8,2,128]{0,3,2,1:T(8,128)(2,1)} %bitcast.80, bf16[128,8,2,128]{3,2,1,0:T(2,128)(2,1)} %reshape.99), kind=kOutput, calls=%fused_computation.5 | convolution fusion | flops 1086322688 | bytes 25960448 | tf_op jit(solution)/shard_map/qhmd,khmd->hmqk/dot_general | solution.py:64
  98.4 5.9 %copy-done.1 = f32[8,2,128,2048]{3,2,1,0:T(8,128)} copy-done((f32[8,2,128,2048]{3,2,1,0:T(8,128)}, f32[8,2,128,2048]{3,2,1,0:T(8,128)S(1)}, u32[]{:S(2)}) %copy-start.1) | copy-done | bytes 16777240
  104.3 5.0 %fusion.1 = f32[8,2,128]{2,1,0:T(2,128)S(1)} fusion(f32[8,2,128,2048]{3,2,1,0:T(8,128)S(1)} %get-tuple-element.21, f32[8,2,128]{2,1,0:T(2,128)S(1)} %broadcast_maximum_fusion, pred[128,2048]{1,0:T(8,128)(4,1)S(1)} %fusion.24), kind=kLoop, calls=%fused_computation.6 | loop fusion | flops 20969472 | bytes 17055744 | tf_op jit(solution)/shard_map/reduce_sum | solution.py:70
  109.3 63.0 %all-gather.7.cloned.1.call-done = bf16[2048,2048]{0,1:T(8,128)(2,1)} async-done(((bf16[128,2048]{0,1:T(8,128)(2,1)}), bf16[2048,2048]{0,1:T(8,128)(2,1)}) %all-gather.7.cloned.1.call-update) | async-done | bytes 8388624 | tf_op jit(solution)/shard_map/all_gather | solution.py:55
  172.3 12.6 %broadcast_divide_fusion = f32[8,2,128,256]{3,2,1,0:T(8,128)S(1)} fusion(f32[8,2,128]{2,1,0:T(2,128)S(1)} %fusion.1, bf16[2048,8,256,1]{0,2,3,1:T(8,128)(2,1)} %bitcast.87, f32[8,2,128,2048]{3,2,1,0:T(8,128)} %copy-done.1, f32[8,2,128]{2,1,0:T(2,128)S(1)} %broadcast_maximum_fusion, pred[128,2048]{1,0:T(8,128)(4,1)S(1)} %fusion.24), kind=kOutput, calls=%fused_computation.36 | convolution fusion | flops 2168979456 | bytes 27541504 | tf_op jit(solution)/shard_map/hmqk,khe->hmqe/dot_general | solution.py:71
  185.1 1.1 fusion.25
  186.2 2.0 copy.42
  188.3 5.7 %fusion.13 = bf16[128,2048]{1,0:T(8,128)(2,1)} fusion(bf16[128,2048]{0,1:T(8,128)(2,1)} %bitcast.85, bf16[2048,2048]{1,0:T(8,128)(2,1)} %param.21, bf16[128,2048]{1,0:T(8,128)(2,1)} %param.15), kind=kOutput, calls=%fused_computation.22 | convolution fusion | flops 1074528256 | bytes 9961472 | tf_op jit(solution)/shard_map/dot_general | solution.py:86
  194.2 31.3 %all-gather.9.cloned.1.call-done = bf16[1024,2048]{1,0:T(8,128)(2,1)} async-done(((bf16[128,2048]{1,0:T(8,128)(2,1)}), bf16[1024,2048]{1,0:T(8,128)(2,1)}) %all-gather.9.cloned.1.call-update) | async-done | bytes 4194320 | tf_op jit(solution)/shard_map/all_gather | solution.py:88
  225.5 3.2 fusion.3
  228.9 6.7 %fusion.15 = f32[1024,704]{0,1:T(8,128)} fusion(bf16[2048,704]{0,1:T(8,128)(2,1)} %param.23, bf16[1024,2048]{1,0:T(8,128)(2,1)S(1)} %copy-done.2, f32[2048]{0:T(1024)S(1)} %copy-done.9, f32[1024]{0:T(1024)S(1)} %add_rsqrt_fusion), kind=kOutput, calls=%fused_computation.26 | convolution fusion | flops 2961178624 | bytes 9973760 | tf_op jit(solution)/shard_map/dot_general | solution.py:90
  235.7 12.4 %convolution_convert_fusion = bf16[1024,2048]{1,0:T(8,128)(2,1)} fusion(bf16[704,2048]{1,0:T(8,128)(2,1)} %param.25, f32[1024,704]{0,1:T(8,128)} %fusion.15, bf16[2048,704]{0,1:T(8,128)(2,1)} %param.24, bf16[1024,2048]{1,0:T(8,128)(2,1)} %all-gather.9.cloned.1.call-done, f32[2048]{0:T(1024)S(1)} %copy-done.9, f32[1024]{0:T(1024)S(1)} %add_rsqrt_fusion), kind=kOutput, calls=%fused_computation.19 | convolution fusion | flops 5920391168 | bytes 17051648 | tf_op jit(solution)/shard_map/dot_general | solution.py:94
  248.1 37.9 %reduce-scatter.2.cloned.1.call-done = bf16[128,2048]{1,0:T(8,128)(2,1)} async-done(((bf16[1024,2048]{1,0:T(8,128)(2,1)}), bf16[128,2048]{1,0:T(8,128)(2,1)}) %reduce-scatter.2.cloned.1.call-update) | async-done | bytes 524304 | tf_op jit(solution)/shard_map/reduce_scatter | solution.py:93
  286.0 1.5 fusion.19
  289.3 31.2 %all-gather.11.cloned.1.call-done = bf16[1024,2048]{1,0:T(8,128)(2,1)} async-done(((bf16[128,2048]{1,0:T(8,128)(2,1)}), bf16[1024,2048]{1,0:T(8,128)(2,1)}) %all-gather.11.cloned.1.call-update) | async-done | bytes 4194320 | tf_op jit(solution)/shard_map/all_gather | solution.py:102
  320.4 5.6 %convolution_convert_fusion.1 = bf16[1024,768]{1,0:T(8,128)(2,1)S(1)} fusion(bf16[1024,2048]{1,0:T(8,128)(2,1)} %all-gather.11.cloned.1.call-done, bf16[2048,768]{1,0:T(8,128)(2,1)S(1)} %copy-done), kind=kOutput, calls=%fused_computation.23 | convolution fusion | flops 3222011904 | bytes 8912896 | tf_op jit(solution)/shard_map/dot_general | solution.py:101
  331.6 4.3 %all-to-all-start = ((bf16[8,128,768]{2,1,0:T(8,128)(2,1)}), bf16[8,128,768]{2,1,0:T(8,128)(2,1)}, u32[]{:S(2)}, u32[]{:S(2)}) async-start(bf16[8,128,768]{2,1,0:T(8,128)(2,1)} %fusion.28), calls=%async_computation.1 | async-start | bytes 3145728 | tf_op jit(solution)/shard_map/all_to_all | solution.py:107
  338.0 1.2 sort.35
  339.2 18.2 %all-to-all-done = bf16[8,128,768]{2,1,0:T(8,128)(2,1)} async-done(((bf16[8,128,768]{2,1,0:T(8,128)(2,1)}), bf16[8,128,768]{2,1,0:T(8,128)(2,1)}, u32[]{:S(2)}, u32[]{:S(2)}) %all-to-all-start) | async-done | bytes 1572896 | tf_op jit(solution)/shard_map/all_to_all | solution.py:107
  357.5 2.6 copy.43
  360.1 2.3 slice.43
  362.3 2.3 copy.45
  364.6 2.8 gather_fusion
  367.4 7.0 %all-to-all-start.1 = ((bf16[16,1,8,4096]{3,2,1,0:T(8,128)(2,1)}), bf16[16,1,8,4096]{3,2,1,0:T(8,128)(2,1)}, u32[]{:S(2)}, u32[]{:S(2)}) async-start(bf16[16,1,8,4096]{3,2,1,0:T(8,128)(2,1)} %bitcast.83), calls=%async_computation.2 | async-start | bytes 2097152 | tf_op jit(solution)/shard_map/all_to_all | solution.py:122
  375.9 1.9 slice.42
  377.8 2.0 copy.47
  379.8 12.0 %all-to-all-done.1 = bf16[16,1,8,4096]{3,2,1,0:T(8,128)(2,1)} async-done(((bf16[16,1,8,4096]{3,2,1,0:T(8,128)(2,1)}), bf16[16,1,8,4096]{3,2,1,0:T(8,128)(2,1)}, u32[]{:S(2)}, u32[]{:S(2)}) %all-to-all-start.1) | async-done | bytes 1048608 | tf_op jit(solution)/shard_map/all_to_all | solution.py:122
  392.9 3.4 scatter_fusion
  (68 shorter events, 13.9 us)
Async XLA Ops:
  7.2 313.3 %copy-start = (bf16[2048,768]{1,0:T(8,128)(2,1)S(1)}, bf16[2048,768]{1,0:T(8,128)(2,1)}, u32[]{:S(2)}) copy-start(bf16[2048,768]{1,0:T(8,128)(2,1)} %param.27) | copy-start | bytes 9437188
  7.2 6.7 %copy-start.6 = (f32[4,128]{1,0:T(4,128)S(1)}, f32[4,128]{1,0:T(4,128)}, u32[]{:S(2)}) copy-start(f32[4,128]{1,0:T(4,128)} %param.20) | copy-start | bytes 6148
  7.2 8.6 %copy-start.5 = (s32[1,2048]{1,0:T(1,128)S(1)}, s32[1,2048]{1,0:T(1,128)}, u32[]{:S(2)}) copy-start(s32[1,2048]{1,0:T(1,128)} %param.19) | copy-start | bytes 24580
  7.2 84.5 %all-gather.5.cloned.1.call-start = ((), (), s32[]{:S(2)}) async-start(), calls=%async_computation.3 | async-start | bytes 8912896 | tf_op jit(solution)/shard_map/all_gather | solution.py:54
  9.5 162.8 %all-gather.7.cloned.1.call-start = ((), (), s32[]{:S(2)}) async-start(), calls=%async_computation.4 | async-start | bytes 8912896 | tf_op jit(solution)/shard_map/all_gather | solution.py:55
  11.6 213.9 %all-gather.9.cloned.1.call-start = ((), (), s32[]{:S(2)}) async-start(), calls=%async_computation.5 | async-start | bytes 4718592 | tf_op jit(solution)/shard_map/all_gather | solution.py:88
  98.4 5.9 %copy-start.1 = (f32[8,2,128,2048]{3,2,1,0:T(8,128)}, f32[8,2,128,2048]{3,2,1,0:T(8,128)S(1)}, u32[]{:S(2)}) copy-start(f32[8,2,128,2048]{3,2,1,0:T(8,128)S(1)} %get-tuple-element.21) | copy-start | bytes 50331652
  193.9 34.8 %copy-start.9 = (f32[2048]{0:T(1024)S(1)}, f32[2048]{0:T(1024)}, u32[]{:S(2)}) copy-start(f32[2048]{0:T(1024)} %param.22) | copy-start | bytes 24580
  193.9 92.0 %reduce-scatter.2.cloned.1.call-start = ((), (), s32[]{:S(2)}) async-start(), calls=%async_computation.6 | async-start | bytes 4718592 | tf_op jit(solution)/shard_map/reduce_scatter | solution.py:93
  225.5 3.4 copy-start.2
  248.1 40.2 %copy-start.4 = (f32[2048]{0:T(1024)S(1)}, f32[2048]{0:T(1024)}, u32[]{:S(2)}) copy-start(f32[2048]{0:T(1024)} %param.26) | copy-start | bytes 24580
  248.1 72.4 %all-gather.11.cloned.1.call-start = ((), (), s32[]{:S(2)}) async-start(), calls=%async_computation.7 | async-start | bytes 4718592 | tf_op jit(solution)/shard_map/all_gather | solution.py:102
  287.5 0.8 copy-start.3
  326.0 10.3 %copy-start.7 = (s32[1,256]{1,0:T(1,128)S(1)}, s32[1,256]{1,0:T(1,128)}, u32[]{:S(2)}) copy-start(s32[1,256]{1,0:T(1,128)} %param.28) | copy-start | bytes 3076
  326.1 11.2 %copy-start.8 = (s32[1,256]{1,0:T(1,128)S(1)}, s32[1,256]{1,0:T(1,128)}, u32[]{:S(2)}) copy-start(s32[1,256]{1,0:T(1,128)} %param.29) | copy-start | bytes 3076
  331.6 25.9 %all-to-all-start = ((bf16[8,128,768]{2,1,0:T(8,128)(2,1)}), bf16[8,128,768]{2,1,0:T(8,128)(2,1)}, u32[]{:S(2)}, u32[]{:S(2)}) async-start(bf16[8,128,768]{2,1,0:T(8,128)(2,1)} %fusion.28), calls=%async_computation.1 | async-start | bytes 3145728 | tf_op jit(solution)/shard_map/all_to_all | solution.py:107
  367.4 24.4 %all-to-all-start.1 = ((bf16[16,1,8,4096]{3,2,1,0:T(8,128)(2,1)}), bf16[16,1,8,4096]{3,2,1,0:T(8,128)(2,1)}, u32[]{:S(2)}, u32[]{:S(2)}) async-start(bf16[16,1,8,4096]{3,2,1,0:T(8,128)(2,1)} %bitcast.83), calls=%async_computation.2 | async-start | bytes 2097152 | tf_op jit(solution)/shard_map/all_to_all | solution.py:122
Sparse Core Ops, SparseCore 0:
  10.7 80.9 all-gather.4
  94.4 77.8 all-gather.6
  194.1 31.3 all-gather.8
  248.2 37.7 reduce-scatter.1
  289.4 31.0 all-gather.10
